TPU v7x, 128 devices: a whole 4x4x4 slice. The times are simulated.
128 devices in a mesh: row: 8 (over x, z_hi), col: 16 (over z_lo, y, core).
Axes of the slice: x: 4, y: 4, z: 4 (z_hi: 2, z_lo: 2; z = z_hi * 2 + z_lo), core: 2. Of those that a mesh axis runs over, the one named last changes fastest.
Arguments:
- window: float32 [12288, 12288], P('row', 'col'), may hold values from -6 to 6
- reflectors: float32 [2, 12288, 256], P(None, 'row', 'col'), may hold values from -0.0546875 to 0.0546875
- factors: float32 [2, 256, 256], replicated, may hold values from -0.375 to 0.375
Outputs:
- updated: float32 [12288, 12288], P('row', 'col')
All inputs are finite; a program needn't handle non-finite values.
Results may differ from a plain program's by a relative error of at most 0.0001.
Values sent between devices are 32-bit elements; how exact they have to be, the bound alone decides.
A program may use at most 128 MiB of HBM per device.

v0:
```python
import jax
import jax.numpy as jnp
from jax import lax
from jax.sharding import PartitionSpec as P

HIGH = lax.Precision.HIGH


def mm(a, b, ca, cb):
    return lax.dot_general(
        a, b, (((ca,), (cb,)), ((), ())), precision=HIGH, preferred_element_type=jnp.float32
    )


def body(window, reflectors, factors):
    panels, rows, piece = reflectors.shape
    cols = window.shape[1]
    row_n = lax.axis_size("row")
    col_n = lax.axis_size("col")
    block = piece * col_n
    width = panels * block
    c = lax.axis_index("col")
    vt = jnp.swapaxes(reflectors, 1, 2)
    vr = lax.all_gather(vt, "col", axis=1, tiled=True).reshape(width, rows)
    halves = vt.reshape(panels, piece, 2, cols)
    k = c % 2
    own = lax.dynamic_index_in_dim(halves, k, 2, keepdims=False)
    other = lax.dynamic_index_in_dim(halves, 1 - k, 2, keepdims=False)
    pairs_a = []
    pairs_b = []
    for r in range(row_n):
        for cc in range(col_n):
            pairs_a.append((r * col_n + cc, cc // 2 * col_n + 2 * r + cc % 2))
            pairs_b.append((r * col_n + cc, cc // 2 * col_n + 2 * r + 1 - cc % 2))
    got_a = lax.ppermute(own, ("row", "col"), pairs_a)
    got_b = lax.ppermute(other, ("row", "col"), pairs_b)
    first = jnp.where(k == 0, got_a, got_b)
    second = jnp.where(k == 0, got_b, got_a)
    pair = jnp.stack([first, second], 1)
    vc = lax.all_gather(pair, "row", axis=1, tiled=True).reshape(width, cols)
    p_part = mm(vr, window, 1, 0)
    y_part = mm(window, vc, 1, 1)
    p_own = lax.psum_scatter(p_part, "row", scatter_dimension=0, tiled=True)
    y_own = lax.psum_scatter(y_part, "col", scatter_dimension=0, tiled=True)
    g12 = lax.psum(mm(vc[:block], vc[block:], 1, 1), "col")
    s_own = lax.psum(mm(p_own, vc, 1, 1), "col")
    t1, t2 = (factors[0], factors[1])
    t12 = -mm(mm(t1, g12, 1, 0), t2, 1, 0)
    tc = jnp.concatenate(
        [jnp.concatenate([t1, t12], 1), jnp.concatenate([jnp.zeros_like(t1), t2], 1)], 0
    )
    p_own = p_own - mm(mm(s_own, tc, 1, 0), vc, 1, 0)
    z_own = mm(y_own, tc, 1, 0)
    p_all = lax.all_gather(p_own, "row", axis=0, tiled=True)
    z_all = lax.all_gather(z_own, "col", axis=0, tiled=True)
    q = mm(tc, p_all, 0, 0)
    return window - mm(vr, q, 0, 0) - mm(z_all, vc, 1, 0)


def solution(mesh):
    placed = (P("row", "col"), P(None, "row", "col"), P())
    return jax.shard_map(
        body, mesh=mesh, in_specs=placed, out_specs=P("row", "col"), check_vma=False
    )
```

profile of v0, /device:TPU:1, one launch (start us, length us, event | category | flops | bytes accessed | tf_op | source)
XLA Modules:
  0.0 484.4 jit_solution(11163545829636249357)
XLA Ops:
  7.3 1.1 reshape.11
  8.6 1.5 collective-permute-start.1
  11.8 44.7 %all-gather.7.cloned.1.call-done = f32[2,256,1536]{2,1,0:T(8,128)} async-done(((f32[2,16,1536]{2,1,0:T(8,128)}), f32[2,256,1536]{2,1,0:T(8,128)}) %all-gather.7.cloned.1.call-update) | async-done | bytes 3145744 | tf_op jit(solution)/shard_map/all_gather | solution.py:24
  56.5 8.5 %fusion.21 = f32[512,768]{1,0:T(8,128)} fusion(f32[512,1536]{1,0:T(8,128)} %bitcast.55, f32[1536,768]{1,0:T(8,128)} %param.3), kind=kOutput, calls=%fused_computation.34 | convolution fusion | flops 3623878656 | bytes 9437184 | tf_op jit(solution)/shard_map/dot_general | solution.py:10
  65.1 42.1 %all-gather.5.cloned.1.call-done = f32[2,16,16,768]{3,2,1,0:T(8,128)} async-done(((f32[2,2,16,768]{3,2,1,0:T(8,128)}), f32[2,16,16,768]{3,2,1,0:T(8,128)}) %all-gather.5.cloned.1.call-update) | async-done | bytes 1572880 | tf_op jit(solution)/shard_map/all_gather | solution.py:40
  107.1 1.6 fusion.18
  108.7 1.2 fusion.20
  110.0 74.3 %reduce-scatter.5.cloned.1.call-done = f32[64,768]{1,0:T(8,128)} async-done(((f32[512,768]{1,0:T(8,128)}), f32[64,768]{1,0:T(8,128)}) %reduce-scatter.5.cloned.1.call-update) | async-done | bytes 196624 | tf_op jit(solution)/shard_map/reduce_scatter | solution.py:43
  184.3 2.4 fusion.22
  186.8 7.9 %convolution_bitcast_fusion = f32[1536,512]{0,1:T(8,128)} fusion(f32[512,768]{1,0:T(8,128)S(1)} %bitcast.52, f32[1536,768]{1,0:T(8,128)} %param.3), kind=kOutput, calls=%fused_computation.2 | convolution fusion | flops 3623878656 | bytes 9437184 | tf_op jit(solution)/shard_map/dot_general | solution.py:10
  194.7 3.6 copy.26
  199.6 106.0 %all-reduce.4.cloned.1.call-done = (f32[64,512]{1,0:T(8,128)}, f32[256,256]{1,0:T(8,128)}) async-done(((f32[64,512]{1,0:T(8,128)}, f32[256,256]{1,0:T(8,128)}), (f32[64,512]{1,0:T(8,128)}, f32[256,256]{1,0:T(8,128)})) %all-reduce.4.cloned.1.call-update) | async-done | bytes 393232 | tf_op jit(solution)/shard_map/psum | solution.py:46
  305.6 1.3 fusion.5
  307.4 1.4 fusion.3
  308.8 1.3 convolution_subtract_fusion
  310.1 60.9 %reduce-scatter.7.cloned.1.call-done = f32[96,512]{1,0:T(8,128)} async-done(((f32[1536,512]{1,0:T(8,128)}), f32[96,512]{1,0:T(8,128)}) %reduce-scatter.7.cloned.1.call-update) | async-done | bytes 196624
  371.0 2.1 fusion.1
  373.2 6.0 %copy.22 = f32[1536,768]{0,1:T(8,128)} copy(f32[1536,768]{1,0:T(8,128)} %param.3) | data formatting | bytes 9437184 | tf_op args[0]
  379.2 45.8 %all-gather.9.cloned.1.call-done = f32[512,768]{1,0:T(8,128)} async-done(((f32[64,768]{1,0:T(8,128)}), f32[512,768]{1,0:T(8,128)}) %all-gather.9.cloned.1.call-update) | async-done | bytes 1572880 | tf_op jit(solution)/shard_map/all_gather | solution.py:54
  425.0 3.0 fusion.2
  428.1 6.3 %fusion.23 = f32[768,1536]{1,0:T(8,128)} fusion(f32[512,768]{1,0:T(8,128)S(1)} %fusion.2, f32[512,1536]{1,0:T(8,128)S(1)} %bitcast.56), kind=kOutput, calls=%fused_computation.36 | convolution fusion | flops 3623878656 | bytes 9437184 | tf_op jit(solution)/shard_map/dot_general | solution.py:10
  434.3 28.2 %all-gather.11.cloned.1.call-done = f32[1536,512]{1,0:T(8,128)} async-done(((f32[96,512]{1,0:T(8,128)}), f32[1536,512]{1,0:T(8,128)}) %all-gather.11.cloned.1.call-update) | async-done | bytes 3145744 | tf_op jit(solution)/shard_map/all_gather | solution.py:55
  462.5 9.0 %fusion = f32[1536,768]{0,1:T(8,128)} fusion(f32[1536,768]{0,1:T(8,128)} %copy.22, f32[768,1536]{1,0:T(8,128)} %fusion.23, f32[1536,512]{1,0:T(8,128)} %all-gather.11.cloned.1.call-done, f32[512,768]{1,0:T(8,128)S(1)} %bitcast.54), kind=kOutput, calls=%fused_computation.1 | convolution fusion | flops 3626237952 | bytes 18874368 | tf_op jit(solution)/shard_map/dot_general | solution.py:10
  471.5 6.0 %copy.24 = f32[1536,768]{1,0:T(8,128)} copy(f32[1536,768]{0,1:T(8,128)} %fusion) | data formatting | bytes 9437184 | tf_op jit(solution)/shard_map/sub | solution.py:57
  (34 shorter events, 4.6 us)
Async XLA Ops:
  6.5 49.9 %all-gather.7.cloned.1.call-start = ((), (), s32[]{:S(2)}) async-start(), calls=%async_computation.3 | async-start | bytes 3342336 | tf_op jit(solution)/shard_map/all_gather | solution.py:24
  7.3 99.9 %all-gather.5.cloned.1.call-start = ((), (), s32[]{:S(2)}) async-start(), calls=%async_computation.2 | async-start | bytes 1769472 | tf_op jit(solution)/shard_map/all_gather | solution.py:40
  8.6 2.4 collective-permute-start.1
  10.1 0.9 collective-permute-start
  11.7 172.5 %reduce-scatter.5.cloned.1.call-start = ((), (), s32[]{:S(2)}) async-start(), calls=%async_computation.4 | async-start | bytes 1769472 | tf_op jit(solution)/shard_map/reduce_scatter | solution.py:43
  65.0 240.6 %all-reduce.4.cloned.1.call-start = ((), (), s32[]{:S(2)}) async-start(), calls=%async_computation.8 | async-start | bytes 786432 | tf_op jit(solution)/shard_map/psum | solution.py:46
  107.1 77.2 %copy-start = (f32[2,16,16,768]{3,2,1,0:T(8,128)S(1)}, f32[2,16,16,768]{3,2,1,0:T(8,128)}, u32[]{:S(2)}) copy-start(f32[2,16,16,768]{3,2,1,0:T(8,128)} %all-gather.5.cloned.1.call-done) | copy-start | bytes 4718596
  186.7 184.3 %reduce-scatter.7.cloned.1.call-start = ((), (), s32[]{:S(2)}) async-start(), calls=%async_computation.7 | async-start | bytes 3342336
  198.3 1.0 copy-start.2
  198.3 110.5 %copy-start.3 = (f32[64,768]{1,0:T(8,128)S(1)}, f32[64,768]{1,0:T(8,128)}, u32[]{:S(2)}) copy-start(f32[64,768]{1,0:T(8,128)} %reduce-scatter.5.cloned.1.call-done) | copy-start | bytes 589828
  198.3 226.7 %all-gather.9.cloned.1.call-start = ((), (), s32[]{:S(2)}) async-start(), calls=%async_computation.5 | async-start | bytes 1769472 | tf_op jit(solution)/shard_map/all_gather | solution.py:54
  310.1 152.4 %all-gather.11.cloned.1.call-start = ((), (), s32[]{:S(2)}) async-start(), calls=%async_computation.6 | async-start | bytes 3342336 | tf_op jit(solution)/shard_map/all_gather | solution.py:55
  425.0 3.0 copy-start.1
Sparse Core Ops, SparseCore 0:
  9.0 47.4 all-gather.6
  58.8 48.2 all-gather.4
  110.9 73.3 reduce-scatter.4
  186.9 118.7 all-reduce.3
  307.9 63.0 reduce-scatter.6
  373.2 51.7 all-gather.8
  426.7 35.7 all-gather.10
where the time goes:
time: 485 us; the launch traced here: 484 us
  waiting for transfers between devices  403 us (83%)
  matrix products  44.8 us (9%)
  local copies, waits for them, and re-layouts  19.6 us (4%)
  between operations  13.6 us (3%)
    psum x1, waiting for transfers between devices, body(): s_own = lax.psum(mm(p_own, vc, 1, 1), 'col')  106 us
    reduce_scatter x1, waiting for transfers between devices, body(): p_own = lax.psum_scatter(p_part, 'row', scatter_dimension=0, tiled=True)  74.3 us
    unnamed x8, waiting for transfers between devices  61.7 us
    all_gather x1, waiting for transfers between devices, body(): p_all = lax.all_gather(p_own, 'row', axis=0, tiled=True)  45.8 us
    dot_general x12, matrix products, mm(): lax.dot_general(a, b, (((ca,), (cb,)), ((), ())), precision=HIGH, preferr...  44.8 us
    all_gather x1, waiting for transfers between devices, body(): vr = lax.all_gather(vt, 'col', axis=1, tiled=True).reshape(width, rows)  44.7 us
    all_gather x1, waiting for transfers between devices, body(): vc = lax.all_gather(pair, 'row', axis=1, tiled=True).reshape(width, cols)  42.1 us
    all_gather x1, waiting for transfers between devices, body(): z_all = lax.all_gather(z_own, 'col', axis=0, tiled=True)  28.2 us
  transfers between devices with their start and end apart: 9, of which 8 were waited for; matrix products, arithmetic and copies ran while one was open for 10% of the time, Pallas kernels for 0%

commit v1 on v0

--- a/solution.py
+++ b/solution.py
@@ -51,7 +51,8 @@
     )
     p_own = p_own - mm(mm(s_own, tc, 1, 0), vc, 1, 0)
     z_own = mm(y_own, tc, 1, 0)
-    p_all = lax.all_gather(p_own, "row", axis=0, tiled=True)
+    sent = jnp.stack([p_own] * lax.axis_size("row"))
+    p_all = jnp.concatenate(lax.all_to_all(sent, "row", 0, 0), axis=0)
     z_all = lax.all_gather(z_own, "col", axis=0, tiled=True)
     q = mm(tc, p_all, 0, 0)
     return window - mm(vr, q, 0, 0) - mm(z_all, vc, 1, 0)

time: 485 us -> 447 us (0.922)
  waiting for transfers between devices: 403 us -> 359 us
  starting transfers between devices: 2.55 us -> 9.17 us
    all_gather x1 -> x0, waiting for transfers between devices: 45.8 us -> none  [body(): p_all = lax.all_gather(p_own, 'row', axis=0, tiled=True)]
    all_gather x1, waiting for transfers between devices: 28.2 us -> 14 us  [body(): z_all = lax.all_gather(z_own, 'col', axis=0, tiled=True)]
    all_to_all x0 -> x1, waiting for transfers between devices: none -> 13.4 us  [body(): p_all = jnp.concatenate(lax.all_to_all(sent, 'row', 0, 0), axis=0)]
    all_to_all x0 -> x1, starting transfers between devices: none -> 6.66 us  [body(): p_all = jnp.concatenate(lax.all_to_all(sent, 'row', 0, 0), axis=0)]
    unnamed x8 -> x7, waiting for transfers between devices: 61.7 us -> 64.4 us
    unnamed x14 -> x20, local copies, waits for them, and re-layouts: 10.7 us -> 10.7 us
where the time goes in v1:
time: 447 us
  waiting for transfers between devices  359 us (80%)
  matrix products  42.9 us (10%)
  local copies, waits for them, and re-layouts  20.9 us (5%)
  between operations  13.7 us (3%)
  starting transfers between devices  9.17 us (2%)
    psum x1, waiting for transfers between devices, body(): s_own = lax.psum(mm(p_own, vc, 1, 1), 'col')  106 us
    reduce_scatter x1, waiting for transfers between devices, body(): p_own = lax.psum_scatter(p_part, 'row', scatter_dimension=0, tiled=True)  74.3 us
    unnamed x7, waiting for transfers between devices  64.4 us
    all_gather x1, waiting for transfers between devices, body(): vr = lax.all_gather(vt, 'col', axis=1, tiled=True).reshape(width, rows)  44.7 us
    dot_general x12, matrix products, mm(): lax.dot_general(a, b, (((ca,), (cb,)), ((), ())), precision=HIGH, preferr...  42.9 us
    all_gather x1, waiting for transfers between devices, body(): vc = lax.all_gather(pair, 'row', axis=1, tiled=True).reshape(width, cols)  42.1 us
    all_gather x1, waiting for transfers between devices, body(): z_all = lax.all_gather(z_own, 'col', axis=0, tiled=True)  14 us
    all_to_all x1, waiting for transfers between devices, body(): p_all = jnp.concatenate(lax.all_to_all(sent, 'row', 0, 0), axis=0)  13.4 us
  transfers between devices with their start and end apart: 9, of which 8 were waited for; matrix products, arithmetic and copies ran while one was open for 10% of the time, Pallas kernels for 0%

profile of v1, /device:TPU:1, one launch (start us, length us, event | category | flops | bytes accessed | tf_op | source)
XLA Modules:
  0.0 446.6 jit_solution(13340877908266000392)
XLA Ops:
  7.3 1.1 reshape.16
  8.6 1.5 collective-permute-start.1
  11.8 44.7 %all-gather.6.cloned.1.call-done = f32[2,256,1536]{2,1,0:T(8,128)} async-done(((f32[2,16,1536]{2,1,0:T(8,128)}), f32[2,256,1536]{2,1,0:T(8,128)}) %all-gather.6.cloned.1.call-update) | async-done | bytes 3145744 | tf_op jit(solution)/shard_map/all_gather | solution.py:24
  56.5 8.5 %fusion.21 = f32[512,768]{1,0:T(8,128)} fusion(f32[512,1536]{1,0:T(8,128)} %bitcast.56, f32[1536,768]{1,0:T(8,128)} %param.3), kind=kOutput, calls=%fused_computation.34 | convolution fusion | flops 3623878656 | bytes 9437184 | tf_op jit(solution)/shard_map/dot_general | solution.py:10
  65.1 42.1 %all-gather.4.cloned.1.call-done = f32[2,16,16,768]{3,2,1,0:T(8,128)} async-done(((f32[2,2,16,768]{3,2,1,0:T(8,128)}), f32[2,16,16,768]{3,2,1,0:T(8,128)}) %all-gather.4.cloned.1.call-update) | async-done | bytes 1572880 | tf_op jit(solution)/shard_map/all_gather | solution.py:40
  107.1 1.6 fusion.18
  108.7 1.3 fusion.20
  110.0 74.3 %reduce-scatter.5.cloned.1.call-done = f32[64,768]{1,0:T(8,128)} async-done(((f32[512,768]{1,0:T(8,128)}), f32[64,768]{1,0:T(8,128)}) %reduce-scatter.5.cloned.1.call-update) | async-done | bytes 196624 | tf_op jit(solution)/shard_map/reduce_scatter | solution.py:43
  184.3 2.4 fusion.22
  186.8 7.9 %convolution_bitcast_fusion = f32[1536,512]{0,1:T(8,128)} fusion(f32[512,768]{1,0:T(8,128)S(1)} %bitcast.53, f32[1536,768]{1,0:T(8,128)} %param.3), kind=kOutput, calls=%fused_computation.2 | convolution fusion | flops 3623878656 | bytes 9437184 | tf_op jit(solution)/shard_map/dot_general | solution.py:10
  194.7 3.6 copy.26
  199.7 106.0 %all-reduce.4.cloned.1.call-done = (f32[64,512]{1,0:T(8,128)}, f32[256,256]{1,0:T(8,128)}) async-done(((f32[64,512]{1,0:T(8,128)}, f32[256,256]{1,0:T(8,128)}), (f32[64,512]{1,0:T(8,128)}, f32[256,256]{1,0:T(8,128)})) %all-reduce.4.cloned.1.call-update) | async-done | bytes 393232 | tf_op jit(solution)/shard_map/psum | solution.py:46
  305.7 1.4 fusion.5
  307.5 63.6 %reduce-scatter.7.cloned.1.call-done = f32[96,512]{1,0:T(8,128)} async-done(((f32[1536,512]{1,0:T(8,128)}), f32[96,512]{1,0:T(8,128)}) %reduce-scatter.7.cloned.1.call-update) | async-done | bytes 196624
  371.1 2.1 fusion.1
  374.4 1.3 stack.11
  375.7 6.7 %all-to-all-start = ((f32[8,64,768]{2,1,0:T(8,128)}), f32[8,64,768]{2,1,0:T(8,128)S(1)}, u32[]{:S(2)}, u32[]{:S(2)}) async-start(f32[8,64,768]{2,1,0:T(8,128)} %stack.11), calls=%async_computation.1 | async-start | bytes 3145728 | tf_op jit(solution)/shard_map/all_to_all | solution.py:55
  382.3 6.1 %copy.22 = f32[1536,768]{0,1:T(8,128)} copy(f32[1536,768]{1,0:T(8,128)} %param.3) | data formatting | bytes 9437184 | tf_op args[0]
  388.4 13.4 %all-to-all-done = f32[8,64,768]{2,1,0:T(8,128)S(1)} async-done(((f32[8,64,768]{2,1,0:T(8,128)}), f32[8,64,768]{2,1,0:T(8,128)S(1)}, u32[]{:S(2)}, u32[]{:S(2)}) %all-to-all-start) | async-done | bytes 1572896 | tf_op jit(solution)/shard_map/all_to_all | solution.py:55
  401.8 2.6 fusion.2
  404.4 6.2 %fusion.23 = f32[768,1536]{1,0:T(8,128)} fusion(f32[512,768]{1,0:T(8,128)S(1)} %fusion.2, f32[512,1536]{1,0:T(8,128)S(1)} %bitcast.57), kind=kOutput, calls=%fused_computation.36 | convolution fusion | flops 3623878656 | bytes 9437184 | tf_op jit(solution)/shard_map/dot_general | solution.py:10
  410.7 14.0 %all-gather.8.cloned.1.call-done = f32[1536,512]{1,0:T(8,128)} async-done(((f32[96,512]{1,0:T(8,128)}), f32[1536,512]{1,0:T(8,128)}) %all-gather.8.cloned.1.call-update) | async-done | bytes 3145744 | tf_op jit(solution)/shard_map/all_gather | solution.py:56
  424.7 9.0 %fusion = f32[1536,768]{0,1:T(8,128)} fusion(f32[1536,768]{0,1:T(8,128)} %copy.22, f32[768,1536]{1,0:T(8,128)} %fusion.23, f32[1536,512]{1,0:T(8,128)} %all-gather.8.cloned.1.call-done, f32[512,768]{1,0:T(8,128)S(1)} %bitcast.55), kind=kOutput, calls=%fused_computation.1 | convolution fusion | flops 3626237952 | bytes 18874368 | tf_op jit(solution)/shard_map/dot_general | solution.py:10
  433.7 6.0 %copy.24 = f32[1536,768]{1,0:T(8,128)} copy(f32[1536,768]{0,1:T(8,128)} %fusion) | data formatting | bytes 9437184 | tf_op jit(solution)/shard_map/sub | solution.py:58
  (40 shorter events, 5.6 us)
Async XLA Ops:
  6.5 49.9 %all-gather.6.cloned.1.call-start = ((), (), s32[]{:S(2)}) async-start(), calls=%async_computation.4 | async-start | bytes 3342336 | tf_op jit(solution)/shard_map/all_gather | solution.py:24
  7.3 99.9 %all-gather.4.cloned.1.call-start = ((), (), s32[]{:S(2)}) async-start(), calls=%async_computation.3 | async-start | bytes 1769472 | tf_op jit(solution)/shard_map/all_gather | solution.py:40
  8.6 2.4 collective-permute-start.1
  10.1 0.9 collective-permute-start
  11.7 172.6 %reduce-scatter.5.cloned.1.call-start = ((), (), s32[]{:S(2)}) async-start(), calls=%async_computation.5 | async-start | bytes 1769472 | tf_op jit(solution)/shard_map/reduce_scatter | solution.py:43
  65.0 240.7 %all-reduce.4.cloned.1.call-start = ((), (), s32[]{:S(2)}) async-start(), calls=%async_computation.8 | async-start | bytes 786432 | tf_op jit(solution)/shard_map/psum | solution.py:46
  107.1 77.2 %copy-start = (f32[2,16,16,768]{3,2,1,0:T(8,128)S(1)}, f32[2,16,16,768]{3,2,1,0:T(8,128)}, u32[]{:S(2)}) copy-start(f32[2,16,16,768]{3,2,1,0:T(8,128)} %all-gather.4.cloned.1.call-done) | copy-start | bytes 4718596
  186.8 184.3 %reduce-scatter.7.cloned.1.call-start = ((), (), s32[]{:S(2)}) async-start(), calls=%async_computation.7 | async-start | bytes 3342336
  198.3 1.0 copy-start.2
  198.3 226.4 %all-gather.8.cloned.1.call-start = ((), (), s32[]{:S(2)}) async-start(), calls=%async_computation.6 | async-start | bytes 3342336 | tf_op jit(solution)/shard_map/all_gather | solution.py:56
  199.5 174.3 %copy-start.3 = (f32[1,256,256]{1,2,0:T(8,128)}, f32[1,256,256]{1,2,0:T(8,128)S(1)}, u32[]{:S(2)}) copy-start(f32[1,256,256]{1,2,0:T(8,128)S(1)} %copy.28) | copy-start | bytes 786436
  199.5 174.3 %copy-start.5 = (f32[64,768]{1,0:T(8,128)S(1)}, f32[64,768]{1,0:T(8,128)}, u32[]{:S(2)}) copy-start(f32[64,768]{1,0:T(8,128)} %reduce-scatter.5.cloned.1.call-done) | copy-start | bytes 589828
  199.7 174.7 %copy-start.4 = (f32[1,256,256]{1,2,0:T(8,128)}, f32[1,256,256]{1,2,0:T(8,128)S(1)}, u32[]{:S(2)}) copy-start(f32[1,256,256]{1,2,0:T(8,128)S(1)} %copy.31) | copy-start | bytes 786436
  305.7 67.6 %copy-start.6 = (f32[64,512]{1,0:T(8,128)S(1)}, f32[64,512]{1,0:T(8,128)}, u32[]{:S(2)}) copy-start(f32[64,512]{1,0:T(8,128)} %get-tuple-element.5) | copy-start | bytes 393220
  375.7 26.1 %all-to-all-start = ((f32[8,64,768]{2,1,0:T(8,128)}), f32[8,64,768]{2,1,0:T(8,128)S(1)}, u32[]{:S(2)}, u32[]{:S(2)}) async-start(f32[8,64,768]{2,1,0:T(8,128)} %stack.11), calls=%async_computation.1 | async-start | bytes 3145728 | tf_op jit(solution)/shard_map/all_to_all | solution.py:55
  401.8 2.6 copy-start.1
Sparse Core Ops, SparseCore 0:
  9.0 47.4 all-gather.5
  58.8 48.2 all-gather.3
  110.9 73.3 reduce-scatter.4
  186.9 118.7 all-reduce.3
  307.9 63.0 reduce-scatter.6
  373.4 51.2 all-gather.7
